TPU v7x, 256 devices: a whole 4x4x8 slice. The times are simulated.
256 devices in a mesh: gx: 32 (over z_hi, x, core), gy: 8 (over z_lo, y).
Axes of the slice: x: 4, y: 4, z: 8 (z_hi: 4, z_lo: 2; z = z_hi * 2 + z_lo), core: 2. Of those that a mesh axis runs over, the one named last changes fastest.
Arguments:
- checkpoint: float32 [19, 256, 2048], P(None, 'gx', 'gy'), as said below
- cotangent: float32 [19, 256, 2048], P(None, 'gx', 'gy'), may hold values from -6 to 6
- blade_area: float32 [1536], replicated, may hold values from 0.5 to 2
- hub_tile: int32 [16], replicated, may hold values from 0 to 255
- point_side: int32 [1536], replicated, may hold values from 0 to 8
- point_local: int32 [1536], replicated, may hold values from 0 to 2047
Outputs:
- grad_checkpoint: float32 [19, 256, 2048], P(None, 'gx', 'gy')
- grad_area: float32 [1536], replicated
Inputs may be any that keep to these rules, and one draw needn't show every extreme that they name: `hub_tile`: tile ids count every tile of the slab. `point_side`: every actuator point lies in its hub tile or one of the eight tiles around it. `checkpoint`: populations are positive and near a local equilibrium with density near one and streamwise velocity near 0.08.
All inputs are finite; a program needn't handle non-finite values.
Results may differ from a plain program's by a relative error of at most 0.0003.
Values sent between devices are 32-bit elements; how exact they have to be, the bound alone decides.
No kernel may reach another device: no remote copies, remote signals or barrier semaphores. Data moves between devices by JAX's collectives and lax.ppermute only.
A program may use at most 128 MiB of HBM per device.

v0:
```python
import jax
import jax.numpy as jnp
import numpy as np
from jax import lax
from jax.sharding import PartitionSpec as P

NZ = 16
STEPS = 4
NTURB = 16
PTS = 96
TAU_ZERO = 0.52
SMAGORINSKY = 0.17 * 0.17
TINY = 1e-10
THRUST = 4.0
GHOST_RATES = np.array([1.05, 1.15, 1.25, 1.35, 1.45, 1.55, 1.65, 1.75, 1.85])


def extended(value, sides, width):
    for axis, dim in sides:
        size, length = (lax.axis_size(axis), value.shape[dim])
        up = [(i, (i + 1) % size) for i in range(size)]
        down = [(j, i) for i, j in up]
        last = lax.slice_in_dim(value, length - width, length, axis=dim)
        first = lax.slice_in_dim(value, 0, width, axis=dim)
        before = lax.ppermute(last, axis, up)
        after = lax.ppermute(first, axis, down)
        value = jnp.concatenate([before, value, after], axis=dim)
    return value


def lattice():
    axis_part = [(1, 0, 0), (-1, 0, 0), (0, 1, 0), (0, -1, 0), (0, 0, 1), (0, 0, -1)]
    edge_part = [
        (1, 1, 0),
        (-1, -1, 0),
        (1, -1, 0),
        (-1, 1, 0),
        (1, 0, 1),
        (-1, 0, -1),
        (1, 0, -1),
        (-1, 0, 1),
        (0, 1, 1),
        (0, -1, -1),
        (0, 1, -1),
        (0, -1, 1),
    ]
    vectors = np.array([(0, 0, 0)] + axis_part + edge_part) * 1.0
    weights = np.array([1.0 / 3.0] + [1.0 / 18.0] * 6 + [1.0 / 36.0] * 12)
    opposite = np.array(
        [int(np.argmin(np.abs(vectors + vectors[column]).sum(1))) for column in range(19)]
    )
    return (vectors, weights, opposite)


def orthonormal(monomials, weights):
    rows = []
    for entry in monomials:
        vector = entry * 1.0
        for sweep in range(2):
            for other in rows:
                vector = vector - np.sum(weights * vector * other) * other
        vector = vector / np.sqrt(np.sum(weights * vector * vector))
        rows.append(vector)
    return np.stack(rows, 0)


def tables():
    vectors, weights, opposite = lattice()
    along_x, along_y, along_z = (vectors[:, 0], vectors[:, 1], vectors[:, 2])
    monomials = [
        np.ones(19),
        along_x,
        along_y,
        along_z,
        along_x * along_x,
        along_y * along_y,
        along_z * along_z,
        along_x * along_y,
        along_x * along_z,
        along_y * along_z,
        along_x * along_y * along_y,
        along_x * along_z * along_z,
        along_y * along_x * along_x,
        along_y * along_z * along_z,
        along_z * along_x * along_x,
        along_z * along_y * along_y,
        along_x * along_x * along_y * along_y,
        along_x * along_x * along_z * along_z,
        along_y * along_y * along_z * along_z,
    ]
    basis = orthonormal(monomials, weights)
    second = weights[:, None] * basis[4:10].T
    ghost = weights[:, None] * basis[10:].T * GHOST_RATES[None, :]
    stress = np.stack(
        [
            along_x * along_x,
            along_y * along_y,
            along_z * along_z,
            along_x * along_y,
            along_x * along_z,
            along_y * along_z,
        ],
        0,
    )
    push = 3.0 * weights * along_x
    return {
        "vectors": vectors,
        "weights": weights,
        "opposite": opposite,
        "high": jnp.asarray(basis[4:], jnp.float32),
        "second": jnp.asarray(second, jnp.float32),
        "ghost": jnp.asarray(ghost, jnp.float32),
        "stress": jnp.asarray(stress, jnp.float32),
        "push": jnp.asarray(push, jnp.float32),
        "velt": jnp.asarray(vectors.T, jnp.float32),
        "wvec": jnp.asarray(weights, jnp.float32),
        "vecs": jnp.asarray(vectors, jnp.float32),
    }


def streamwise_velocity(flat, table):
    density = jnp.sum(flat, 0)
    momentum = jnp.dot(table["velt"], flat, precision=lax.Precision.HIGHEST)
    return momentum[0] / density


def collide(flat, force, table):
    density = jnp.sum(flat, 0)
    momentum = jnp.dot(table["velt"], flat, precision=lax.Precision.HIGHEST)
    velocity = momentum / density[None, :]
    project = jnp.dot(table["vecs"], velocity, precision=lax.Precision.HIGHEST)
    speed_sq = jnp.sum(velocity * velocity, 0)
    equil = (
        table["wvec"][:, None]
        * density[None, :]
        * (1.0 + 3.0 * project + 4.5 * project * project - 1.5 * speed_sq[None, :])
    )
    noneq = flat - equil
    stress = jnp.dot(table["stress"], noneq, precision=lax.Precision.HIGHEST)
    square = jnp.sum(stress[:3] * stress[:3], 0) + 2.0 * jnp.sum(stress[3:] * stress[3:], 0)
    relax_time = 0.5 * (
        TAU_ZERO
        + jnp.sqrt(TAU_ZERO * TAU_ZERO + 18.0 * SMAGORINSKY * jnp.sqrt(square + TINY) / density)
    )
    moments = jnp.dot(table["high"], noneq, precision=lax.Precision.HIGHEST)
    relaxed = jnp.dot(
        table["second"], moments[:6] / relax_time[None, :], precision=lax.Precision.HIGHEST
    )
    relaxed = relaxed + jnp.dot(table["ghost"], moments[6:], precision=lax.Precision.HIGHEST)
    return flat - relaxed + table["push"][:, None] * force[None, :]


def wall_mask(vectors, depth):
    keep = np.ones((19, depth))
    for column in range(19):
        if vectors[column, 2] > 0.5:
            keep[column, 0] = 0.0
        if vectors[column, 2] < -0.5:
            keep[column, depth - 1] = 0.0
    return keep


def neighbours(field, vectors, direction):
    pops, width_x, span = field.shape
    depth = NZ
    width_y = span // depth
    step_x = [int(direction * vectors[column, 0]) for column in range(19)]
    step_y = [int(direction * vectors[column, 1]) for column in range(19)]
    step_z = [int(direction * vectors[column, 2]) for column in range(19)]
    padded = extended(field.reshape(pops, width_x, width_y, depth), (("gx", 1), ("gy", 2)), 1)
    padded = padded.reshape(pops, width_x + 2, (width_y + 2) * depth)
    padded = jnp.pad(padded, ((0, 0), (0, 0), (1, 1)))
    pieces = []
    for column in range(19):
        start_x = 1 - step_x[column]
        start_j = depth + 1 - step_y[column] * depth - step_z[column]
        pieces.append(padded[column, start_x : start_x + width_x, start_j : start_j + span])
    return jnp.stack(pieces, 0)


def turbine_total(partial_value):
    return lax.psum(partial_value, ("gx", "gy"))


def body(checkpoint, cotangent, blade_area, hub_tile, point_side, point_local):
    table = tables()
    vectors = table["vectors"]
    opposite = table["opposite"]
    pops, width_x, span = checkpoint.shape
    width_y = span // NZ
    cells = width_x * span
    keep = jnp.asarray(np.tile(wall_mask(vectors, NZ), (1, width_y)), jnp.float32)[:, None, :]
    count_x = lax.axis_size("gx")
    count_y = lax.axis_size("gy")
    index_x = lax.axis_index("gx")
    index_y = lax.axis_index("gy")
    turbine = jnp.arange(NTURB * PTS, dtype=jnp.int32) // PTS
    hub_x = hub_tile // count_y
    hub_y = hub_tile % count_y
    tile_x = (hub_x[turbine] + point_side // 3 - 1) % count_x
    tile_y = (hub_y[turbine] + point_side % 3 - 1) % count_y
    mine = ((tile_x == index_x) & (tile_y == index_y)).astype(jnp.float32)
    denom = jnp.sum(blade_area.reshape(NTURB, PTS), 1)

    def stream_adjoint(adjoint):
        pushed = neighbours(adjoint * keep, vectors, -1)
        return pushed + ((1.0 - keep) * adjoint)[opposite]

    def collide_local(flat, force):
        return collide(flat, force, table)

    def velocity_local(flat):
        return streamwise_velocity(flat, table)

    field = checkpoint
    saved = []
    for counter in range(STEPS):
        flat = (neighbours(field, vectors, 1) * keep + (1.0 - keep) * field[opposite]).reshape(
            pops, cells
        )
        sampled = velocity_local(flat)[point_local] * mine
        numer = turbine_total(jnp.sum((blade_area * sampled).reshape(NTURB, PTS), 1))
        rotor = numer / denom
        thrust = -THRUST * blade_area * rotor[turbine] * sampled
        force = jnp.zeros((cells,), jnp.float32).at[point_local].add(thrust)
        saved.append((flat, sampled, rotor, force))
        field = collide_local(flat, force).reshape(pops, width_x, span)
    adjoint = cotangent
    area_grad = jnp.zeros_like(blade_area)
    for counter in range(STEPS - 1, -1, -1):
        flat, sampled, rotor, force = saved[counter]
        unused, pullback = jax.vjp(collide_local, flat, force)
        flat_bar, force_bar = pullback(adjoint.reshape(pops, cells))
        thrust_bar = force_bar[point_local] * mine
        rotor_here = rotor[turbine]
        sample_bar = thrust_bar * -THRUST * blade_area * rotor_here
        rotor_part = jnp.sum((thrust_bar * -THRUST * blade_area * sampled).reshape(NTURB, PTS), 1)
        rotor_bar = turbine_total(rotor_part)
        numer_bar = rotor_bar / denom
        sample_bar = sample_bar + numer_bar[turbine] * blade_area * mine
        area_grad = area_grad + thrust_bar * -THRUST * rotor_here * sampled
        area_grad = area_grad + mine * rotor_bar[turbine] * (sampled - rotor_here) / denom[turbine]
        speed_bar = jnp.zeros((cells,), jnp.float32).at[point_local].add(sample_bar)
        unused_speed, speed_pull = jax.vjp(velocity_local, flat)
        flat_bar = flat_bar + speed_pull(speed_bar)[0]
        adjoint = stream_adjoint(flat_bar.reshape(pops, width_x, span))
    grad_area = lax.psum(area_grad, ("gx", "gy"))
    return (adjoint, grad_area)


def solution(mesh):
    return jax.shard_map(
        body,
        mesh=mesh,
        in_specs=(P(None, "gx", "gy"), P(None, "gx", "gy"), P(), P(), P(), P()),
        out_specs=(P(None, "gx", "gy"), P()),
        check_vma=False,
    )
```

profile of v0, /device:TPU:1, one launch (start us, length us, event | category | flops | bytes accessed | tf_op | source)
XLA Modules:
  0.0 1147.3 jit_solution(11894280306716798596)
XLA Ops:
  7.4 8.9 select_reduce_fusion.13
  38.4 11.2 fusion.199
  49.9 82.5 %psum.63 = f32[16]{0:T(128)S(1)} all-reduce(f32[16]{0:T(128)S(1)} %reduce_sum.414), channel_id=1, replica_groups=mesh['gx'=32,'gy'=8] {'gx','gy'}, use_global_device_ids=true, to_apply=%region_5.6 | all-reduce | flops 16 | bytes 128 | tf_op jit(solution)/shard_map/psum | solution.py:182
  143.3 8.7 scatter_custom_fusion
  172.3 8.4 gather_fusion.3
  181.3 84.2 %psum.64 = f32[16]{0:T(128)S(1)} all-reduce(f32[16]{0:T(128)S(1)} %reduce_sum.426), channel_id=1, replica_groups=mesh['gx'=32,'gy'=8] {'gx','gy'}, use_global_device_ids=true, to_apply=%region_13.14 | all-reduce | flops 16 | bytes 128 | tf_op jit(solution)/shard_map/psum | solution.py:182
  276.4 8.8 scatter_custom_fusion.1
  314.6 84.7 %psum.65 = f32[16]{0:T(128)S(1)} all-reduce(f32[16]{0:T(128)S(1)} %reduce_sum.434), channel_id=1, replica_groups=mesh['gx'=32,'gy'=8] {'gx','gy'}, use_global_device_ids=true, to_apply=%region_20.21 | all-reduce | flops 16 | bytes 128 | tf_op jit(solution)/shard_map/psum | solution.py:182
  410.3 8.8 scatter_custom_fusion.2
  421.1 11.7 %gather_fusion.7 = f32[1536]{0:T(1024)} fusion(f32[2048]{0:T(1024)S(1)} %bitcast.826, s32[2048]{0:T(1024)S(1)} %copy-done.21), kind=kCustom, calls=%fused_computation.7 | custom fusion | bytes 18432 | tf_op jit(solution)/shard_map/gather | solution.py:234
  465.3 81.7 %all-reduce.28 = (f32[16]{0:T(128)S(1)}, f32[16]{0:T(128)S(1)}) all-reduce(f32[16]{0:T(128)S(1)} %reduce_sum.455, f32[16]{0:T(128)S(1)} %reduce_sum.454), channel_id=1, replica_groups=mesh['gx'=32,'gy'=8] {'gx','gy'}, use_global_device_ids=true, to_apply=%region_34.35 | all-reduce | flops 32 | bytes 256 | tf_op jit(solution)/shard_map/psum | solution.py:182
  557.5 11.6 %fusion.186 = f32[1536]{0:T(1024)S(1)} fusion(pred[1536]{0:T(1024)(128)(4,1)S(1)} %copy-done.69, f32[1536]{0:T(1024)S(1)} %copy-done.5, pred[1536]{0:T(1024)(128)(4,1)S(1)} %copy-done.76, pred[1536]{0:T(1024)(128)(4,1)S(1)} %copy-done.84, pred[1536]{0:T(1024)(128)(4,1)S(1)} %copy-done.92, pred[1536]{0:T(1024)(128)(4,1)S(1)} %copy-done.100, ...), kind=kLoop, calls=%fused_computation.541 | loop fusion | flops 38400 | bytes 46152 | tf_op jit(solution)/shard_map/add | solution.py:240
  569.1 8.8 scatter_custom_fusion.3
  609.6 80.4 %psum.68 = f32[16]{0:T(128)S(1)} all-reduce(f32[16]{0:T(128)S(1)} %reduce_sum.468), channel_id=1, replica_groups=mesh['gx'=32,'gy'=8] {'gx','gy'}, use_global_device_ids=true, to_apply=%region_42.43 | all-reduce | flops 16 | bytes 128 | tf_op jit(solution)/shard_map/psum | solution.py:182
  697.6 11.3 fusion.184
  708.9 8.8 scatter_custom_fusion.4
  748.6 80.9 %psum.69 = f32[16]{0:T(128)S(1)} all-reduce(f32[16]{0:T(128)S(1)} %reduce_sum.478), channel_id=1, replica_groups=mesh['gx'=32,'gy'=8] {'gx','gy'}, use_global_device_ids=true, to_apply=%region_50.51 | all-reduce | flops 16 | bytes 128 | tf_op jit(solution)/shard_map/psum | solution.py:182
  837.3 11.3 fusion.182
  848.6 8.8 scatter_custom_fusion.5
  888.2 81.0 %psum.70 = f32[16]{0:T(128)S(1)} all-reduce(f32[16]{0:T(128)S(1)} %reduce_sum.491), channel_id=1, replica_groups=mesh['gx'=32,'gy'=8] {'gx','gy'}, use_global_device_ids=true, to_apply=%region_58.59 | all-reduce | flops 16 | bytes 128 | tf_op jit(solution)/shard_map/psum | solution.py:182
  977.0 11.2 fusion.180
  988.2 8.8 scatter_custom_fusion.6
  1009.5 50.7 %fusion.166 = f32[1536]{0:T(1024)S(1)} fusion(pred[1536]{0:T(1024)(128)(4,1)S(1)} %copy-done.72, pred[1536]{0:T(1024)(128)(4,1)S(1)} %copy-done.80, pred[1536]{0:T(1024)(128)(4,1)S(1)} %copy-done.88, pred[1536]{0:T(1024)(128)(4,1)S(1)} %copy-done.96, pred[1536]{0:T(1024)(128)(4,1)S(1)} %copy-done.104, pred[1536]{0:T(1024)(128)(4,1)S(1)} %copy-done.112, ...), kind=kLoop, calls=%fused_computation.513 | loop fusion | flops 190464 | bytes 126276 | tf_op jit(solution)/shard_map/add | solution.py:242
  1061.0 80.0 %psum.71 = f32[1536]{0:T(1024)} all-reduce(f32[1536]{0:T(1024)S(1)} %fusion.166), channel_id=1, replica_groups=mesh['gx'=32,'gy'=8] {'gx','gy'}, use_global_device_ids=true, to_apply=%region_60.61 | all-reduce | flops 1536 | bytes 12288 | tf_op jit(solution)/shard_map/psum | solution.py:247
  (1192 shorter events, 286.5 us)
Async XLA Ops:
  2.0 14.3 %collective-permute-start = (f32[19,1,16,16]{3,2,1,0:T(8,128)S(1)}, f32[19,1,16,16]{3,2,1,0:T(8,128)S(1)}, u32[]{:S(2)}, u32[]{:S(2)}) collective-permute-start(f32[19,1,16,16]{3,2,1,0:T(8,128)S(1)} %get-tuple-element.69), channel_id=1, source_target_pairs={{0,8},{8,16},{16,24},{24,32},{32,40},{40,48},{48,56},{56,64},{64,7... | collective-permute-start | bytes 58376 | tf_op jit(solution)/shard_map/ppermute | solution.py:25
  4.7 11.8 %collective-permute-start.1 = (f32[19,1,16,16]{3,2,1,0:T(8,128)S(1)}, f32[19,1,16,16]{3,2,1,0:T(8,128)S(1)}, u32[]{:S(2)}, u32[]{:S(2)}) collective-permute-start(f32[19,1,16,16]{3,2,1,0:T(8,128)S(1)} %get-tuple-element.68), channel_id=1, source_target_pairs={{8,0},{16,8},{24,16},{32,24},{40,32},{48,40},{56,48},{64,56},{72,6... | collective-permute-start | bytes 58376 | tf_op jit(solution)/shard_map/ppermute | solution.py:26
  17.8 5.6 collective-permute-start.2
  18.5 5.0 collective-permute-start.3
  153.9 4.7 collective-permute-start.5
  158.8 6.6 collective-permute-start.6
  159.3 6.1 collective-permute-start.7
  287.4 4.7 collective-permute-start.9
  292.2 6.5 collective-permute-start.10
  293.3 5.4 collective-permute-start.11
  420.3 13.6 %collective-permute-start.12 = (f32[19,1,16,16]{3,2,1,0:T(8,128)S(1)}, f32[19,1,16,16]{3,2,1,0:T(8,128)S(1)}, u32[]{:S(2)}, u32[]{:S(2)}) collective-permute-start(f32[19,1,16,16]{3,2,1,0:T(8,128)S(1)} %get-tuple-element.63), channel_id=1, source_target_pairs={{0,8},{8,16},{16,24},{24,32},{32,40},{40,48},{48,56},{56,64},{64,7... | collective-permute-start | bytes 58376 | tf_op jit(solution)/shard_map/ppermute | solution.py:25
  432.8 4.7 collective-permute-start.13
  438.8 10.4 collective-permute-start.14
  439.3 9.9 collective-permute-start.15
  586.0 9.1 collective-permute-start.18
  586.1 9.0 collective-permute-start.19
  725.5 8.8 collective-permute-start.22
  725.6 8.7 collective-permute-start.23
  865.0 8.9 collective-permute-start.26
  865.0 8.8 collective-permute-start.27
  999.1 6.4 collective-permute-start.28
  1000.1 5.3 collective-permute-start.29
  1005.7 135.3 %collective-permute-start.30 = (f32[19,10,1,16]{3,2,1,0:T(1,128)S(1)}, f32[19,10,1,16]{3,2,1,0:T(1,128)S(1)}, u32[]{:S(2)}, u32[]{:S(2)}) collective-permute-start(f32[19,10,1,16]{3,2,1,0:T(1,128)S(1)} %get-tuple-element.38), channel_id=1, source_target_pairs={{0,1},{1,2},{2,3},{3,4},{4,5},{5,6},{6,7},{7,0},{8,9},{9,10},{10,1... | collective-permute-start | bytes 36488 | tf_op jit(solution)/shard_map/ppermute | solution.py:25
  1005.9 135.1 %collective-permute-start.31 = (f32[19,10,1,16]{3,2,1,0:T(1,128)S(1)}, f32[19,10,1,16]{3,2,1,0:T(1,128)S(1)}, u32[]{:S(2)}, u32[]{:S(2)}) collective-permute-start(f32[19,10,1,16]{3,2,1,0:T(1,128)S(1)} %get-tuple-element.39), channel_id=1, source_target_pairs={{1,0},{2,1},{3,2},{4,3},{5,4},{6,5},{7,6},{0,7},{9,8},{10,9},{11,1... | collective-permute-start | bytes 36488 | tf_op jit(solution)/shard_map/ppermute | solution.py:26
  (283 other events, 11701.1 us)
where the time goes:
time: 1160 us; the launch traced here: 1150 us
  blocking collectives  655 us (56%)
  other arithmetic  277 us (24%)
  local copies, waits for them, and re-layouts  125 us (11%)
  starting transfers between devices  41.8 us (4%)
  waiting for transfers between devices  23 us (2%)
  matrix products  17.3 us (1%)
    psum x7, blocking collectives, turbine_total(): return lax.psum(partial_value, ('gx', 'gy'))  575 us
    psum x1, blocking collectives, body(): grad_area = lax.psum(area_grad, ('gx', 'gy'))  80 us
    add x1, other arithmetic, body(): area_grad + mine * rotor_bar[turbine] * (sampled - rotor_here) / denom[tu...  50.7 us
    add x4, other arithmetic, body(): sample_bar = sample_bar + numer_bar[turbine] * blade_area * mine  45.4 us
    gather x4, local copies, waits for them, and re-layouts, body(): thrust_bar = force_bar[point_local] * mine  36.9 us
    scatter-add x4, other arithmetic, body(): speed_bar = jnp.zeros((cells,), jnp.float32).at[point_local].add(sample_bar)  35.2 us
    gather x4, local copies, waits for them, and re-layouts, body(): sampled = velocity_local(flat)[point_local] * mine  33.6 us
    ppermute x16, starting transfers between devices, extended(): after = lax.ppermute(first, axis, down)  30.8 us
  transfers between devices with their start and end apart: 32, of which 14 were waited for; matrix products, arithmetic and copies ran while one was open for 10% of the time, Pallas kernels for 0%

commit v1 on v0

--- a/solution.py
+++ b/solution.py
@@ -13,6 +13,12 @@
 TINY = 1e-10
 THRUST = 4.0
 GHOST_RATES = np.array([1.05, 1.15, 1.25, 1.35, 1.45, 1.55, 1.65, 1.75, 1.85])
+
+
+def summed_here(value, axis):
+    blocks = lax.all_gather(value, axis, axis=0, tiled=False)
+    total = blocks.sum(axis=0)
+    return total
 
 
 def extended(value, sides, width):
@@ -244,7 +250,7 @@
         unused_speed, speed_pull = jax.vjp(velocity_local, flat)
         flat_bar = flat_bar + speed_pull(speed_bar)[0]
         adjoint = stream_adjoint(flat_bar.reshape(pops, width_x, span))
-    grad_area = lax.psum(area_grad, ("gx", "gy"))
+    grad_area = summed_here(area_grad, ("gx", "gy"))
     return (adjoint, grad_area)
 
 

time: 1160 us -> 1780 us (1.53)
  waiting for transfers between devices: 23 us -> 701 us
  blocking collectives: 655 us -> 575 us
    all_gather x0 -> x1, waiting for transfers between devices: none -> 677 us  [summed_here(): blocks = lax.all_gather(value, axis, axis=0, tiled=False)]
    psum x1 -> x0, blocking collectives: 80 us -> none  [body(): grad_area = lax.psum(area_grad, ('gx', 'gy'))]
  transfers between devices with their start and end apart: 32 -> 33, of which waited for: 14 -> 16; matrix products, arithmetic and copies ran while one was open for 10% -> 7% of each run, Pallas kernels for 0% -> 0%
where the time goes in v1:
time: 1780 us; the launch traced here: 1760 us
  waiting for transfers between devices  701 us (39%)
  blocking collectives  575 us (32%)
  other arithmetic  280 us (16%)
  local copies, waits for them, and re-layouts  125 us (7%)
  starting transfers between devices  42.1 us (2%)
  between operations  21.3 us (1%)
    all_gather x1, waiting for transfers between devices, summed_here(): blocks = lax.all_gather(value, axis, axis=0, tiled=False)  677 us
    psum x7, blocking collectives, turbine_total(): return lax.psum(partial_value, ('gx', 'gy'))  575 us
    add x1, other arithmetic, body(): area_grad + mine * rotor_bar[turbine] * (sampled - rotor_here) / denom[tu...  50.8 us
    add x4, other arithmetic, body(): sample_bar = sample_bar + numer_bar[turbine] * blade_area * mine  45.4 us
    gather x4, local copies, waits for them, and re-layouts, body(): thrust_bar = force_bar[point_local] * mine  36.9 us
  transfers between devices with their start and end apart: 33, of which 16 were waited for; matrix products, arithmetic and copies ran while one was open for 7% of the time, Pallas kernels for 0%

profile of v1, /device:TPU:1, one launch (start us, length us, event | category | flops | bytes accessed | tf_op | source)
XLA Modules:
  0.0 1762.9 jit_solution(18349628436391774068)
XLA Ops:
  14.0 8.9 select_reduce_fusion.13
  36.6 8.4 gather_fusion.1
  45.0 11.2 fusion.199
  56.5 82.5 %psum.56 = f32[16]{0:T(128)S(1)} all-reduce(f32[16]{0:T(128)S(1)} %reduce_sum.422), channel_id=1, replica_groups=mesh['gx'=32,'gy'=8] {'gx','gy'}, use_global_device_ids=true, to_apply=%region_5.6 | all-reduce | flops 16 | bytes 128 | tf_op jit(solution)/shard_map/psum | solution.py:188
  149.8 8.7 scatter_custom_fusion
  187.8 84.2 %psum.57 = f32[16]{0:T(128)S(1)} all-reduce(f32[16]{0:T(128)S(1)} %reduce_sum.434), channel_id=1, replica_groups=mesh['gx'=32,'gy'=8] {'gx','gy'}, use_global_device_ids=true, to_apply=%region_13.14 | all-reduce | flops 16 | bytes 128 | tf_op jit(solution)/shard_map/psum | solution.py:188
  283.1 8.8 scatter_custom_fusion.1
  321.4 84.6 %psum.58 = f32[16]{0:T(128)S(1)} all-reduce(f32[16]{0:T(128)S(1)} %reduce_sum.442), channel_id=1, replica_groups=mesh['gx'=32,'gy'=8] {'gx','gy'}, use_global_device_ids=true, to_apply=%region_20.21 | all-reduce | flops 16 | bytes 128 | tf_op jit(solution)/shard_map/psum | solution.py:188
  416.8 8.8 scatter_custom_fusion.2
  427.5 11.7 gather_fusion.7
  471.5 81.7 %all-reduce.28 = (f32[16]{0:T(128)S(1)}, f32[16]{0:T(128)S(1)}) all-reduce(f32[16]{0:T(128)S(1)} %reduce_sum.463, f32[16]{0:T(128)S(1)} %reduce_sum.462), channel_id=1, replica_groups=mesh['gx'=32,'gy'=8] {'gx','gy'}, use_global_device_ids=true, to_apply=%region_34.35 | all-reduce | flops 32 | bytes 256 | tf_op jit(solution)/shard_map/psum | solution.py:188
  563.8 11.5 fusion.186
  575.3 8.8 scatter_custom_fusion.3
  615.7 80.4 %psum.61 = f32[16]{0:T(128)S(1)} all-reduce(f32[16]{0:T(128)S(1)} %reduce_sum.476), channel_id=1, replica_groups=mesh['gx'=32,'gy'=8] {'gx','gy'}, use_global_device_ids=true, to_apply=%region_42.43 | all-reduce | flops 16 | bytes 128 | tf_op jit(solution)/shard_map/psum | solution.py:188
  703.9 11.1 fusion.184
  715.0 8.8 scatter_custom_fusion.4
  754.8 80.9 %psum.62 = f32[16]{0:T(128)S(1)} all-reduce(f32[16]{0:T(128)S(1)} %reduce_sum.489), channel_id=1, replica_groups=mesh['gx'=32,'gy'=8] {'gx','gy'}, use_global_device_ids=true, to_apply=%region_50.51 | all-reduce | flops 16 | bytes 128 | tf_op jit(solution)/shard_map/psum | solution.py:188
  843.4 11.4 fusion.182
  854.8 8.8 scatter_custom_fusion.5
  894.5 81.0 %psum.63 = f32[16]{0:T(128)S(1)} all-reduce(f32[16]{0:T(128)S(1)} %reduce_sum.499), channel_id=1, replica_groups=mesh['gx'=32,'gy'=8] {'gx','gy'}, use_global_device_ids=true, to_apply=%region_58.59 | all-reduce | flops 16 | bytes 128 | tf_op jit(solution)/shard_map/psum | solution.py:188
  984.0 11.4 fusion.180
  995.4 8.8 scatter_custom_fusion.6
  1012.1 50.8 %fusion.166 = f32[1536]{0:T(1024)S(1)} fusion(pred[1536]{0:T(1024)(128)(4,1)S(1)} %copy-done.72, pred[1536]{0:T(1024)(128)(4,1)S(1)} %copy-done.80, pred[1536]{0:T(1024)(128)(4,1)S(1)} %copy-done.88, pred[1536]{0:T(1024)(128)(4,1)S(1)} %copy-done.96, pred[1536]{0:T(1024)(128)(4,1)S(1)} %copy-done.104, pred[1536]{0:T(1024)(128)(4,1)S(1)} %copy-done.112, ...), kind=kLoop, calls=%fused_computation.513 | loop fusion | flops 190464 | bytes 126276 | tf_op jit(solution)/shard_map/add | solution.py:248
  1075.4 677.2 %all-gather.4.cloned.1.call-done = f32[256,1,1536]{2,1,0:T(1,128)} async-done(((f32[1,1,1536]{2,1,0:T(1,128)}), f32[256,1,1536]{2,1,0:T(1,128)}) %all-gather.4.cloned.1.call-update) | async-done | bytes 1572880 | tf_op jit(solution)/shard_map/all_gather | solution.py:19
  (1192 shorter events, 291.2 us)
Async XLA Ops:
  7.2 1745.5 %all-gather.4.cloned.1.call-start = ((), (), s32[]{:S(2)}) async-start(), calls=%async_computation | async-start | bytes 1579008 | tf_op jit(solution)/shard_map/all_gather | solution.py:19
  8.6 14.4 collective-permute-start
  11.2 11.9 collective-permute-start.1
  24.4 5.6 collective-permute-start.2
  25.1 5.0 collective-permute-start.3
  160.4 4.7 collective-permute-start.5
  165.3 6.6 collective-permute-start.6
  165.8 6.1 collective-permute-start.7
  294.2 4.7 collective-permute-start.9
  299.0 6.5 collective-permute-start.10
  300.0 5.4 collective-permute-start.11
  426.7 13.6 collective-permute-start.12
  445.2 10.2 collective-permute-start.14
  445.8 9.6 collective-permute-start.15
  592.2 9.1 collective-permute-start.18
  592.3 9.0 collective-permute-start.19
  731.6 8.8 collective-permute-start.22
  731.7 8.7 collective-permute-start.23
  871.3 8.9 collective-permute-start.26
  871.4 8.8 collective-permute-start.27
  1006.3 57.3 %collective-permute-start.28 = (f32[19,1,16,16]{3,2,1,0:T(8,128)S(1)}, f32[19,1,16,16]{3,2,1,0:T(8,128)S(1)}, u32[]{:S(2)}, u32[]{:S(2)}) collective-permute-start(f32[19,1,16,16]{3,2,1,0:T(8,128)S(1)} %get-tuple-element.54), channel_id=1, source_target_pairs={{0,8},{8,16},{16,24},{24,32},{32,40},{40,48},{48,56},{56,64},{64,7... | collective-permute-start | bytes 58376 | tf_op jit(solution)/shard_map/ppermute | solution.py:31
  1007.3 56.3 %collective-permute-start.29 = (f32[19,1,16,16]{3,2,1,0:T(8,128)S(1)}, f32[19,1,16,16]{3,2,1,0:T(8,128)S(1)}, u32[]{:S(2)}, u32[]{:S(2)}) collective-permute-start(f32[19,1,16,16]{3,2,1,0:T(8,128)S(1)} %get-tuple-element.55), channel_id=1, source_target_pairs={{8,0},{16,8},{24,16},{32,24},{40,32},{48,40},{56,48},{64,56},{72,6... | collective-permute-start | bytes 58376 | tf_op jit(solution)/shard_map/ppermute | solution.py:32
  1063.8 5.6 collective-permute-start.30
  1064.0 5.4 collective-permute-start.31
  (282 other events, 11682.7 us)
Sparse Core Ops, SparseCore 0:
  1063.6 689.0 all-gather.3
